TPU v7x, 128 devices: a whole 4x4x4 slice. The times are simulated.
128 devices in a mesh: layer: 4 (over x_hi, core), tok: 32 (over z, x_lo, y).
Axes of the slice: x: 4 (x_hi: 2, x_lo: 2; x = x_hi * 2 + x_lo), y: 4, z: 4, core: 2. Of those that a mesh axis runs over, the one named last changes fastest.
Arguments:
- kv_cache: bfloat16 [4, 2, 2, 1, 16384, 1024], P('layer', None, None, None, 'tok'), may hold values from -6 to 6
- keep_mask: int32 [4, 1, 16384], P('layer', None, 'tok'), may hold values 0 or 1
- lengths: int32 [1], replicated, may hold values from 4096 to 16384
Outputs:
- decode_cache: bfloat16 [1, 8, 8, 2, 16384, 128], P(None, 'layer', None, None, 'tok')
Inputs may be any that keep to these rules, and one draw needn't show every extreme that they name: `keep_mask`: 1 keeps the token of both layers of the pair unmerged. `lengths`: positions at or past a sequence's length are padding.
All inputs are finite; a program needn't handle non-finite values. No bound on the sum of `keep_mask` on one device may be relied on, other than what follows from the above.
Results may differ from a plain program's by a relative error of at most 0.001.
Values may be sent and summed in bfloat16 or wider, within the bound.
A program may use at most 64 MiB of HBM per device.

v0:
```python
import jax
import jax.numpy as jnp
from jax import lax
from jax.sharding import PartitionSpec as P

KVH = 8
HD = 128
PAGE = 16


epsilon = 1e-06


def merge_pair(lower_layer, upper_layer, retained, inside):
    lower_scale = jnp.sqrt(jnp.mean(lower_layer * lower_layer, axis=-1, keepdims=True) + epsilon)
    upper_scale = jnp.sqrt(jnp.mean(upper_layer * upper_layer, axis=-1, keepdims=True) + epsilon)
    summed = lower_layer / lower_scale + upper_layer / upper_scale
    direction = summed / jnp.sqrt(jnp.mean(summed * summed, axis=-1, keepdims=True) + epsilon)
    lower_out = jnp.where(retained, lower_layer, lower_scale * direction)
    upper_out = jnp.where(retained, upper_layer, upper_scale * direction)
    lower_out = jnp.where(inside, lower_out, jnp.zeros_like(lower_out))
    upper_out = jnp.where(inside, upper_out, jnp.zeros_like(upper_out))
    return jnp.stack([lower_out, upper_out], axis=0).astype(jnp.bfloat16)


def shards(kv_cache, keep_mask, lengths):
    groups = lax.axis_size("layer")
    tok_count = lax.axis_size("tok")
    seq_count = kv_cache.shape[3]
    rows_dev = kv_cache.shape[4]
    head_group = KVH // groups
    round_group = rows_dev // (PAGE * tok_count)
    offset = lax.axis_index("tok") * rows_dev
    position = offset + jnp.arange(rows_dev, dtype=jnp.int32)
    inside = (position[None, :] < lengths[:, None])[None, :, :, None, None]
    retained = (keep_mask[0] > 0)[None, :, :, None, None]
    values = kv_cache[0].astype(jnp.float32).reshape(2, 2, seq_count, rows_dev, KVH, HD)
    merged = merge_pair(values[0], values[1], retained, inside)
    outgoing = merged.reshape(2, 2, seq_count, round_group, tok_count, PAGE, groups, head_group, HD)
    outgoing = outgoing.transpose(6, 4, 2, 7, 0, 1, 3, 5, 8)
    flat = outgoing.reshape((groups * tok_count,) + outgoing.shape[2:])
    arrived = lax.all_to_all(
        flat, ("layer", "tok"), split_axis=0, concat_axis=0, tiled=True
    ).reshape(outgoing.shape)
    result = arrived.transpose(2, 3, 0, 4, 5, 1, 6, 7, 8)
    return result.reshape(seq_count, head_group, 2 * groups, 2, rows_dev, HD)


def solution(mesh):
    in_specs = (P("layer", None, None, None, "tok", None), P("layer", None, "tok"), P())
    out_specs = P(None, "layer", None, None, "tok", None)
    return jax.shard_map(shards, mesh=mesh, in_specs=in_specs, out_specs=out_specs, check_vma=False)
```

profile of v0, /device:TPU:1, one launch (start us, length us, event | category | flops | bytes accessed | tf_op | source)
XLA Modules:
  0.0 161.4 jit_solution(11699606578438191119)
XLA Ops:
  0.0 5.1 %fusion.7 = (f32[1,1,2,1,512,1024]{5,4,3,2,1,0:T(8,128)S(1)}, f32[1,1,2,1,512,1024]{5,4,3,2,1,0:T(8,128)}) fusion(bf16[1,2,2,1,512,1024]{5,4,3,2,1,0:T(8,128)(2,1)} %param.3), kind=kLoop, calls=%fused_computation.19 | loop fusion | bytes 16777216 | tf_op jit(solution)/shard_map/slice | solution.py:38
  5.1 0.0 copy-start.3
  5.1 1.0 copy.59
  6.1 1.0 copy-done.3
  7.1 0.0 copy-start.1
  7.1 2.0 %copy-done.1 = f32[128,8,8,128]{3,2,1,0:T(8,128)} copy-done((f32[128,8,8,128]{3,2,1,0:T(8,128)}, f32[128,8,8,128]{3,2,1,0:T(8,128)S(1)}, u32[]{:S(2)}) %copy-start.1) | copy-done | bytes 4194328
  9.1 1.1 multiply_reduce_fusion.1
  10.3 0.2 copy.43
  10.5 0.2 copy.47
  10.7 0.1 sqrt.39
  10.8 3.2 %copy.58 = f32[128,8,8,128]{3,2,1,0:T(8,128)S(1)} copy(f32[128,8,8,128]{3,1,2,0:T(8,128)} %bitcast.78) | data formatting | bytes 8388608
  14.0 0.0 copy-start.2
  14.0 1.9 %copy-done.2 = f32[128,8,8,128]{3,2,1,0:T(8,128)} copy-done((f32[128,8,8,128]{3,2,1,0:T(8,128)}, f32[128,8,8,128]{3,2,1,0:T(8,128)S(1)}, u32[]{:S(2)}) %copy-start.2) | copy-done | bytes 4194328
  16.0 1.1 multiply_reduce_fusion.2
  17.1 0.2 copy.40
  17.3 0.2 copy.46
  17.5 0.1 sqrt.37
  17.6 6.8 %squeeze.14 = f32[1,2,32,16,4,2,128]{6,5,4,0,3,2,1:T(2,128)} reshape(f32[1,1,2,1,512,1024]{5,4,3,2,1,0:T(8,128)} %copy-done.3) | data formatting | bytes 8388608 | tf_op jit(solution)/shard_map/squeeze | solution.py:38
  24.4 6.6 %squeeze.12 = f32[1,2,32,16,4,2,128]{6,5,4,0,3,2,1:T(2,128)} reshape(f32[1,1,2,1,512,1024]{5,4,3,2,1,0:T(8,128)} %get-tuple-element.8) | data formatting | bytes 8388608 | tf_op jit(solution)/shard_map/squeeze | solution.py:38
  31.0 17.2 %multiply_reduce_fusion = f32[2,512,8]{2,1,0:T(8,128)S(1)} fusion(f32[2,1,512,8,128]{4,3,2,0,1:T(8,128)} %bitcast.75, f32[2,1,512,8,128]{4,3,2,0,1:T(8,128)} %bitcast.77, f32[2,512,8]{2,1,0:T(8,128)S(1)} %copy.47, f32[2,512,8]{2,1,0:T(8,128)S(1)} %copy.46), kind=kLoop, calls=%fused_computation.8 | loop fusion | flops 5234688 | bytes 8486912 | tf_op jit(solution)/shard_map/reduce_sum | solution.py:18
  48.2 0.0 copy-start.4
  48.2 0.2 copy.48
  48.4 0.1 sqrt.41
  48.5 2.6 %copy.49 = f32[2,32,16,4,2]{4,3,2,1,0:T(4,128)} copy(f32[2,32,16,4,2]{2,1,4,3,0:T(8,128)S(1)} %sqrt.41) | data formatting | bytes 65536 | tf_op jit(solution)/shard_map/sqrt | solution.py:18
  51.1 1.7 %copy.44 = f32[2,32,16,4,2]{4,3,2,1,0:T(4,128)S(1)} copy(f32[2,32,16,4,2]{2,1,4,3,0:T(8,128)S(1)} %sqrt.39) | data formatting | bytes 65536 | tf_op jit(solution)/shard_map/sqrt | solution.py:16
  52.8 2.6 %copy.41 = f32[2,32,16,4,2]{4,3,2,1,0:T(4,128)} copy(f32[2,32,16,4,2]{2,1,4,3,0:T(8,128)S(1)} %sqrt.37) | data formatting | bytes 65536 | tf_op jit(solution)/shard_map/sqrt | solution.py:15
  56.1 0.0 copy-done.4
  56.1 0.1 gt.18
  56.3 0.0 copy-start
  56.3 20.2 %fusion.5 = (bf16[1,2,1,1,32,16,4,2,128]{8,7,6,5,4,1,3,2,0:T(2,128)(2,1)}, f32[1,2,32,16,4,2,128]{6,5,4,3,2,1,0:T(2,128)S(1)}) fusion(f32[1,2,32,16,4,2,128]{6,5,4,0,3,2,1:T(2,128)} %squeeze.12, f32[2,32,16,4,2]{4,3,2,1,0:T(4,128)} %copy.41, pred[32,16]{1,0:T(8,128)(4,1)S(1)} %gt.18, pred[32,16]{1,0:T(8,128)(4,1)S(1)} %add_compare_fusion, ...), kind=kLoop, calls=%fused_computation.13 | loop fusion | flops 7340032 | bytes 14779392 | tf_op jit(solution)/shard_map/stack | solution.py:23
  76.4 0.0 copy-done
  76.4 8.1 %fusion.4 = bf16[1,2,1,1,32,16,4,2,128]{8,7,6,5,4,1,3,2,0:T(2,128)(2,1)} fusion(f32[1,2,32,16,4,2,128]{6,5,4,3,2,1,0:T(2,128)S(1)} %get-tuple-element.6, f32[2,32,16,4,2]{4,3,2,1,0:T(4,128)S(1)} %copy.44, f32[1,2,32,16,4,2,128]{6,5,4,0,3,2,1:T(2,128)S(1)} %copy-done, pred[32,16]{1,0:T(8,128)(4,1)S(1)} %gt.18, pred[32,16]{1,0:T(8,128)(4,1)S(1)} %add_compare_fusion), kind=kLoop, calls=%fused_computation.12 | loop fusion | flops 3145728 | bytes 10519552 | tf_op jit(solution)/shard_map/stack | solution.py:23
  84.5 8.5 %maximum_bitcast_fusion = bf16[4,32,1,2,2,2,1,16,128]{8,3,0,7,1,5,6,2,4:T(2,128)(2,1)S(1)} fusion(bf16[1,2,1,1,32,16,4,2,128]{8,7,6,5,4,1,3,2,0:T(2,128)(2,1)} %fusion.4, bf16[1,2,1,1,32,16,4,2,128]{8,7,6,5,4,1,3,2,0:T(2,128)(2,1)} %get-tuple-element.5), kind=kLoop, calls=%fused_computation.4 | loop fusion | flops 2097152 | bytes 8388608 | tf_op jit(solution)/shard_map/transpose | solution.py:40
  93.0 1.3 copy.55
  94.3 64.0 %all_to_all.5 = bf16[128,1,2,2,2,1,16,128]{7,6,4,3,2,5,1,0:T(8,128)(2,1)S(1)} all-to-all(bf16[128,1,2,2,2,1,16,128]{7,6,4,3,2,5,1,0:T(8,128)(2,1)S(1)} %bitcast.80), channel_id=1, replica_groups=mesh['layer'=4,'tok'=32] {'layer','tok'}, dimensions={0} | all-to-all | bytes 8388608 | tf_op jit(solution)/shard_map/all_to_all | solution.py:42
  158.3 3.1 %copy.57 = bf16[1,2,4,2,2,32,1,16,128]{8,7,5,4,3,2,1,6,0:T(8,128)(2,1)} copy(bf16[1,2,4,2,2,32,1,16,128]{8,7,4,3,1,5,2,6,0:T(8,128)(2,1)S(1)} %bitcast.81) | data formatting | bytes 8388608 | tf_op jit(solution)/shard_map/transpose | solution.py:45
  (5 shorter events, 0.1 us)
Async XLA Ops:
  5.1 2.1 %copy-start.3 = (f32[1,1,2,1,512,1024]{5,4,3,2,1,0:T(8,128)}, f32[1,1,2,1,512,1024]{5,4,3,2,1,0:T(8,128)S(1)}, u32[]{:S(2)}) copy-start(f32[1,1,2,1,512,1024]{5,4,3,2,1,0:T(8,128)S(1)} %get-tuple-element.7) | copy-start | bytes 12582916
  7.1 2.0 %copy-start.1 = (f32[128,8,8,128]{3,2,1,0:T(8,128)}, f32[128,8,8,128]{3,2,1,0:T(8,128)S(1)}, u32[]{:S(2)}) copy-start(f32[128,8,8,128]{3,2,1,0:T(8,128)S(1)} %copy.59) | copy-start | bytes 12582916
  14.0 2.0 %copy-start.2 = (f32[128,8,8,128]{3,2,1,0:T(8,128)}, f32[128,8,8,128]{3,2,1,0:T(8,128)S(1)}, u32[]{:S(2)}) copy-start(f32[128,8,8,128]{3,2,1,0:T(8,128)S(1)} %copy.58) | copy-start | bytes 12582916
  48.2 8.0 %copy-start.4 = (s32[1,1,512]{2,1,0:T(1,128)S(1)}, s32[1,1,512]{2,1,0:T(1,128)}, u32[]{:S(2)}) copy-start(s32[1,1,512]{2,1,0:T(1,128)} %param.4) | copy-start | bytes 6148
  56.3 20.2 %copy-start = (f32[1,2,32,16,4,2,128]{6,5,4,0,3,2,1:T(2,128)S(1)}, f32[1,2,32,16,4,2,128]{6,5,4,0,3,2,1:T(2,128)}, u32[]{:S(2)}) copy-start(f32[1,2,32,16,4,2,128]{6,5,4,0,3,2,1:T(2,128)} %squeeze.14) | copy-start | bytes 12582916
where the time goes:
time: 162 us; the launch traced here: 161 us
  blocking collectives  64 us (40%)
  other arithmetic  56.3 us (35%)
  local copies, waits for them, and re-layouts  40.2 us (25%)
    all_to_all x1, blocking collectives, shards(): lax.all_to_all(flat, ('layer', 'tok'), split_axis=0, concat_axis=0, tiled...  64 us
    another operation x2, other arithmetic, merge_pair(): return jnp.stack([lower_out, upper_out], axis=0).astype(jnp.bfloat16)  28.2 us
    reduce_sum x1, other arithmetic, merge_pair(): jnp.mean(summed * summed, axis=-1, keepdims=True) + epsilon  17.2 us
    squeeze x2, local copies, waits for them, and re-layouts, shards(): merged = merge_pair(values[0], values[1], retained, inside)  13.3 us
    unnamed x12, local copies, waits for them, and re-layouts  9.18 us
    transpose x1, other arithmetic, shards(): outgoing = outgoing.transpose(6, 4, 2, 7, 0, 1, 3, 5, 8)  8.51 us
    slice x1, local copies, waits for them, and re-layouts, shards(): merged = merge_pair(values[0], values[1], retained, inside)  5.08 us

commit v1 on v0

v1 whole, which is shorter than its diff:
```python
import functools
import itertools

import jax
import jax.numpy as jnp
from jax import lax
from jax.experimental import pallas as pl
from jax.experimental.pallas import tpu as pltpu
from jax.sharding import PartitionSpec as P

KVH = 8
HD = 128
PAGE = 16
EPS = 1e-06
MESH = pl.DeviceIdType.MESH
CHUNKS = [(1, 1, 1), (0, 1, 1), (1, 0, 1), (1, 1, 0), (0, 0, 1), (0, 1, 0), (1, 0, 0), (0, 0, 0)]


def place():
    layer = lax.axis_index("layer")
    tok = lax.axis_index("tok")
    x = (layer // 2) * 2 + (tok // 4) % 2
    return layer, tok, x, tok % 4, tok // 8, layer % 2


def target(x, y, z, core):
    return (x // 2) * 2 + core, z * 8 + (x % 2) * 4 + y


def sends_of(chunk):
    px, py, pz = chunk
    out = []
    for dc in (0, 1):
        for sy, sz in ((0, 0), (0, 2), (2, 0), (2, 2)):
            o = (px, py + sy, pz + sz)
            n = (px + 2, (py + 2 - sy) if py else py + sy, (pz + 2 - sz) if pz else pz + sz)
            out += [o + (dc,), n + (dc,)]
    assert len(set(out)) == 16
    return out


def merge(in_v, keep_v, move_v, buf, k, at):
    zl, xl, yl = at
    def body(step, carry):
        h, c = step // 2, step % 2
        cols = pl.ds(pl.multiple_of(h * HD, HD), HD)
        a = in_v[k, 0, c, :, :, :, cols].reshape(64, HD).astype(jnp.float32)
        b = in_v[k, 1, c, :, :, :, cols].reshape(64, HD).astype(jnp.float32)
        keep = keep_v[:, zl, xl, :, yl].reshape(64, HD)
        move = move_v[:, zl, xl, :, yl].reshape(64, HD)
        ma = jnp.sum(a * a, axis=-1, keepdims=True) * (1.0 / HD) + EPS
        mb = jnp.sum(b * b, axis=-1, keepdims=True) * (1.0 / HD) + EPS
        ia, ib = lax.rsqrt(ma), lax.rsqrt(mb)
        u = a * ia + b * ib
        mu = jnp.sum(u * u, axis=-1, keepdims=True) * (1.0 / HD) + EPS
        s = move * lax.rsqrt(mu)
        lower = (keep * a + (s * (ma * ia)) * u).astype(jnp.bfloat16)
        upper = (keep * b + (s * (mb * ib)) * u).astype(jnp.bfloat16)
        for zh, yh in itertools.product(range(2), range(2)):
            first = (zh * 2 + yh) * PAGE
            block = (zh * 16 + zl * 8 + xl * 4 + yh * 2 + yl) * 4 + h // 2
            buf[block, h % 2, 0, c] = lower[first : first + PAGE]
            buf[block, h % 2, 1, c] = upper[first : first + PAGE]
        return carry

    lax.fori_loop(0, 2 * KVH, body, 0, unroll=2)


def kernel(len_ref, mask_ref, kv_ref, out_ref, in_v, keep_v, move_v, buf, load_sem, own_sem, send_sem, recv_sem):
    layer, tok, x, y, z, core = place()
    everyone = [o for o in itertools.product(range(4), range(4), range(4), range(2)) if any(o)]

    def to(o):
        return target((x + o[0]) % 4, (y + o[1]) % 4, (z + o[2]) % 4, (core + o[3]) % 2)

    def at(chunk):
        px, py, pz = chunk
        return (z + pz) % 2, (x + px) % 2, (y + py) % 2

    loads = []
    for k, chunk in enumerate(CHUNKS):
        zl, xl, yl = at(chunk)
        load = pltpu.make_async_copy(kv_ref.at[:, :, :, zl, xl, :, yl], in_v.at[k], load_sem.at[k])
        load.start()
        loads.append(load)

    barrier = pltpu.get_barrier_semaphore()
    for o in everyone:
        pl.semaphore_signal(barrier, inc=1, device_id=to(o), device_id_type=MESH)

    limit = len_ref[0]
    square = (128, 128)
    diagonal = lax.broadcasted_iota(jnp.int32, square, 0) == lax.broadcasted_iota(jnp.int32, square, 1)
    for k in range(4):
        mask = jnp.broadcast_to(mask_ref[:, k * 128 : (k + 1) * 128], square)
        kept = jnp.sum(jnp.where(diagonal & (mask > 0), 1.0, 0.0), axis=-1, keepdims=True)
        position = tok * 512 + k * 128 + lax.broadcasted_iota(jnp.int32, square, 0)
        inside = jnp.where(position < limit, 1.0, 0.0)
        keep_v[k // 2, k % 2] = (kept * inside).reshape(2, 2, 2, PAGE, HD)
        move_v[k // 2, k % 2] = ((1.0 - kept) * inside).reshape(2, 2, 2, PAGE, HD)

    slots = pl.ds(pl.multiple_of(tok * PAGE, PAGE), PAGE)
    here = out_ref.at[0, :, pl.ds(layer * 2, 2), :, slots, :]

    def block(o):
        there = to(o)
        return there, buf.at[there[1] * 4 + there[0]]

    def send(chunk):
        for o in sends_of(chunk):
            there, data = block(o)
            if any(o):
                pltpu.make_async_remote_copy(
                    src_ref=data, dst_ref=here, send_sem=send_sem, recv_sem=recv_sem,
                    device_id=there, device_id_type=MESH,
                ).start()
            else:
                pltpu.make_async_copy(data, here, own_sem).start()

    for k, chunk in enumerate(CHUNKS):
        loads[k].wait()
        merge(in_v, keep_v, move_v, buf, k, at(chunk))
        if k == 0:
            pl.semaphore_wait(barrier, len(everyone))
            send(chunk)
        if k > 1:
            send(CHUNKS[k - 1])
    send(CHUNKS[-1])

    pltpu.make_async_copy(block((0, 0, 0, 0))[1], here, own_sem).wait()
    rest = buf.at[pl.ds(0, 127)]
    pltpu.make_async_copy(rest, rest, send_sem).wait()
    pltpu.make_async_copy(rest, rest, recv_sem).wait()


def shards(kv_cache, keep_mask, lengths):
    return pl.pallas_call(
        kernel,
        out_shape=jax.ShapeDtypeStruct((1, 2, 8, 2, 512, HD), jnp.bfloat16),
        in_specs=[
            pl.BlockSpec(memory_space=pltpu.SMEM),
            pl.BlockSpec(memory_space=pltpu.VMEM),
            pl.BlockSpec(memory_space=pl.ANY),
        ],
        out_specs=pl.BlockSpec(memory_space=pl.ANY),
        scratch_shapes=[
            pltpu.VMEM((8, 2, 2, 2, 2, PAGE, KVH * HD), jnp.bfloat16),
            pltpu.VMEM((2, 2, 2, 2, 2, PAGE, HD), jnp.float32),
            pltpu.VMEM((2, 2, 2, 2, 2, PAGE, HD), jnp.float32),
            pltpu.VMEM((128, 2, 2, 2, PAGE, HD), jnp.bfloat16),
            pltpu.SemaphoreType.DMA((8,)),
            pltpu.SemaphoreType.DMA,
            pltpu.SemaphoreType.DMA,
            pltpu.SemaphoreType.DMA,
        ],
        compiler_params=pltpu.CompilerParams(collective_id=0, has_side_effects=True),
    )(lengths, keep_mask.reshape(1, 512), kv_cache.reshape(2, 2, 2, 2, 2, 2, 2, PAGE, KVH * HD))


def solution(mesh):
    in_specs = (P("layer", None, None, None, "tok", None), P("layer", None, "tok"), P())
    out_specs = P(None, "layer", None, None, "tok", None)
    return jax.shard_map(shards, mesh=mesh, in_specs=in_specs, out_specs=out_specs, check_vma=False)
```

time: 162 us -> 67.9 us (0.42)
  blocking collectives: 64 us -> 0 us
  Pallas kernels: 0 us -> 62.4 us
  other arithmetic: 56.3 us -> 0 us
  local copies, waits for them, and re-layouts: 40.2 us -> 4.65 us
    all_to_all x1 -> x0, blocking collectives: 64 us -> none  [shards(): lax.all_to_all(flat, ('layer', 'tok'), split_axis=0, concat_axis=0, tiled...]
    pallas_call x0 -> x1, Pallas kernels: none -> 62.4 us  [shards(): pl.pallas_call(kernel, out_shape=jax.ShapeDtypeStruct((1, 2, 8, 2, 512, H...]
    another operation x2 -> x0, other arithmetic: 28.2 us -> none  [merge_pair(): return jnp.stack([lower_out, upper_out], axis=0).astype(jnp.bfloat16)]
    reduce_sum x3 -> x0, other arithmetic: 19.5 us -> none  [the longest x1 17.2 us: merge_pair(): jnp.mean(summed * summed, axis=-1, keepdims=True) + epsilon]
    squeeze x2 -> x0, local copies, waits for them, and re-layouts: 13.3 us -> none  [shards(): merged = merge_pair(values[0], values[1], retained, inside)]
    transpose x1 -> x0, other arithmetic: 8.51 us -> none  [shards(): outgoing = outgoing.transpose(6, 4, 2, 7, 0, 1, 3, 5, 8)]
    sqrt x8 -> x0, local copies, waits for them, and re-layouts: 7.73 us -> none  [the longest x3 2.96 us: merge_pair(): jnp.sqrt(jnp.mean(lower_layer * lower_layer, axis=-1, keepdims=True) + ep...]
    slice x1 -> x0, local copies, waits for them, and re-layouts: 5.08 us -> none  [shards(): merged = merge_pair(values[0], values[1], retained, inside)]
where the time goes in v1:
time: 67.9 us; the launch traced here: 67.7 us
  Pallas kernels  62.4 us (92%)
  local copies, waits for them, and re-layouts  4.65 us (7%)
    pallas_call x1, Pallas kernels, shards(): pl.pallas_call(kernel, out_shape=jax.ShapeDtypeStruct((1, 2, 8, 2, 512, H...  62.4 us
    unnamed x1, local copies, waits for them, and re-layouts  4.65 us

profile of v1, /device:TPU:1, one launch (start us, length us, event | category | flops | bytes accessed | tf_op | source)
XLA Modules:
  0.0 67.7 jit_solution(16651086458528722774)
XLA Ops:
  0.7 62.4 %shard_map.37 = bf16[1,2,8,2,512,128]{5,4,3,2,1,0:T(8,128)(2,1)} custom-call(s32[1]{0:T(128)S(6)} %copy.5.len_ref, s32[1,512]{1,0:T(1,128)} %bitcast.3, bf16[2,2,2,2,2,2,2,16,1024]{8,7,6,5,4,3,2,1,0:T(8,128)(2,1)} %bitcast.2), custom_call_target="tpu_custom_call" | custom-call | tf_op jit(solution)/shard_map/pallas_call | solution.py:137
  63.1 4.7 %copy.6 = bf16[1,2,8,2,512,128]{5,4,3,2,1,0:T(8,128)(2,1)} copy(bf16[1,2,8,2,512,128]{5,4,3,2,1,0:T(8,128)(2,1)} %shard_map.37) | data formatting | bytes 8388608

commit v2 on v1

--- a/solution.py
+++ b/solution.py
@@ -13,7 +13,7 @@
 PAGE = 16
 EPS = 1e-06
 MESH = pl.DeviceIdType.MESH
-CHUNKS = [(1, 1, 1), (0, 1, 1), (1, 0, 1), (1, 1, 0), (0, 0, 1), (0, 1, 0), (1, 0, 0), (0, 0, 0)]
+CHUNKS = [(1, 1, 1), (0, 0, 0), (0, 1, 1), (1, 0, 0), (1, 0, 1), (0, 1, 0), (1, 1, 0), (0, 0, 1)]
 
 
 def place():
@@ -31,7 +31,7 @@
     px, py, pz = chunk
     out = []
     for dc in (0, 1):
-        for sy, sz in ((0, 0), (0, 2), (2, 0), (2, 2)):
+        for sy, sz in ((0, 0), (2, 2), (2, 0), (0, 2)):
             o = (px, py + sy, pz + sz)
             n = (px + 2, (py + 2 - sy) if py else py + sy, (pz + 2 - sz) if pz else pz + sz)
             out += [o + (dc,), n + (dc,)]
@@ -133,16 +133,26 @@
     pltpu.make_async_copy(rest, rest, recv_sem).wait()
 
 
+def put_out(in_ref, out_ref, sem):
+    copies = []
+    for h, j in itertools.product(range(2), range(8)):
+        copies.append(pltpu.make_async_copy(in_ref.at[0, h, j], out_ref.at[0, h, j], sem.at[h * 8 + j]))
+    for copy in copies:
+        copy.start()
+    for copy in copies:
+        copy.wait()
+
+
 def shards(kv_cache, keep_mask, lengths):
-    return pl.pallas_call(
+    landed = pl.pallas_call(
         kernel,
-        out_shape=jax.ShapeDtypeStruct((1, 2, 8, 2, 512, HD), jnp.bfloat16),
+        out_shape=pltpu.VMEM((1, 2, 8, 2, 512, HD), jnp.bfloat16),
         in_specs=[
             pl.BlockSpec(memory_space=pltpu.SMEM),
             pl.BlockSpec(memory_space=pltpu.VMEM),
-            pl.BlockSpec(memory_space=pl.ANY),
+            pl.BlockSpec(memory_space=pltpu.HBM),
         ],
-        out_specs=pl.BlockSpec(memory_space=pl.ANY),
+        out_specs=pl.BlockSpec(memory_space=pltpu.VMEM),
         scratch_shapes=[
             pltpu.VMEM((8, 2, 2, 2, 2, PAGE, KVH * HD), jnp.bfloat16),
             pltpu.VMEM((2, 2, 2, 2, 2, PAGE, HD), jnp.float32),
@@ -153,8 +163,16 @@
             pltpu.SemaphoreType.DMA,
             pltpu.SemaphoreType.DMA,
         ],
-        compiler_params=pltpu.CompilerParams(collective_id=0, has_side_effects=True),
+        compiler_params=pltpu.CompilerParams(collective_id=0, has_side_effects=True, vmem_limit_bytes=58 << 20),
     )(lengths, keep_mask.reshape(1, 512), kv_cache.reshape(2, 2, 2, 2, 2, 2, 2, PAGE, KVH * HD))
+    return pl.pallas_call(
+        put_out,
+        out_shape=jax.ShapeDtypeStruct((1, 2, 8, 2, 512, HD), jnp.bfloat16),
+        in_specs=[pl.BlockSpec(memory_space=pltpu.VMEM)],
+        out_specs=pl.BlockSpec(memory_space=pl.ANY),
+        scratch_shapes=[pltpu.SemaphoreType.DMA((16,))],
+        compiler_params=pltpu.CompilerParams(vmem_limit_bytes=16 << 20),
+    )(landed)
 
 
 def solution(mesh):

time: 67.9 us -> 63.4 us (0.934)
  local copies, waits for them, and re-layouts: 4.65 us -> 0 us
    unnamed x1 -> x0, local copies, waits for them, and re-layouts: 4.65 us -> none
    pallas_call x1 -> x2, Pallas kernels: 62.4 us -> 62.4 us  [the longest x1 60.2 us: shards(): pl.pallas_call(kernel, out_shape=pltpu.VMEM((1, 2, 8, 2, 512, HD), jnp.bf...]
where the time goes in v2:
time: 63.4 us; the launch traced here: 63 us
  Pallas kernels  62.4 us (98%)
  between operations  0.66 us (1%)
    pallas_call x1, Pallas kernels, shards(): pl.pallas_call(kernel, out_shape=pltpu.VMEM((1, 2, 8, 2, 512, HD), jnp.bf...  60.2 us
    pallas_call x1, Pallas kernels, shards(): pl.pallas_call(put_out, out_shape=jax.ShapeDtypeStruct((1, 2, 8, 2, 512,...  2.14 us

profile of v2, /device:TPU:1, one launch (start us, length us, event | category | flops | bytes accessed | tf_op | source)
XLA Modules:
  0.0 63.0 jit_solution(8230456949845322009)
XLA Ops:
  0.7 60.2 %shard_map.37.in_ref = bf16[1,2,8,2,512,128]{5,4,3,2,1,0:T(8,128)(2,1)S(1)} custom-call(s32[1]{0:T(128)S(6)} %copy.4.len_ref, s32[1,512]{1,0:T(1,128)} %bitcast.3, bf16[2,2,2,2,2,2,2,16,1024]{8,7,6,5,4,3,2,1,0:T(8,128)(2,1)} %bitcast.2), custom_call_target="tpu_custom_call" | custom-call | tf_op jit(solution)/shard_map/pallas_call | solution.py:147
  60.9 2.1 %shard_map.38 = bf16[1,2,8,2,512,128]{5,4,3,2,1,0:T(8,128)(2,1)} custom-call(bf16[1,2,8,2,512,128]{5,4,3,2,1,0:T(8,128)(2,1)S(1)} %shard_map.37.in_ref), custom_call_target="tpu_custom_call" | custom-call | tf_op jit(solution)/shard_map/pallas_call | solution.py:168

commit v3 on v2

--- a/solution.py
+++ b/solution.py
@@ -23,8 +23,8 @@
     return layer, tok, x, tok % 4, tok // 8, layer % 2
 
 
-def target(x, y, z, core):
-    return (x // 2) * 2 + core, z * 8 + (x % 2) * 4 + y
+def hops(o):
+    return sum(min(v, 4 - v) for v in o[:3])
 
 
 def sends_of(chunk):
@@ -63,15 +63,22 @@
             buf[block, h % 2, 1, c] = upper[first : first + PAGE]
         return carry
 
-    lax.fori_loop(0, 2 * KVH, body, 0, unroll=2)
+    lax.fori_loop(0, 2 * KVH, body, 0, unroll=8)
 
 
-def kernel(len_ref, mask_ref, kv_ref, out_ref, in_v, keep_v, move_v, buf, load_sem, own_sem, send_sem, recv_sem):
+def kernel(len_ref, mask_hbm, kv_ref, out_ref, mask_ref, in_v, keep_v, move_v, buf, load_sem, own_sem, send_sem, recv_sem):
     layer, tok, x, y, z, core = place()
     everyone = [o for o in itertools.product(range(4), range(4), range(4), range(2)) if any(o)]
+    everyone = sorted(everyone, key=hops, reverse=True)
+
+    xs, ys, zs = ([lax.rem(v + d, 4) for d in range(4)] for v in (x, y, z))
+    cores = [core, 1 - core]
+    to_layer = [[lax.div(v, 2) * 2 + c for c in cores] for v in xs]
+    to_xy = [[lax.rem(v, 2) * 4 + w for w in ys] for v in xs]
 
     def to(o):
-        return target((x + o[0]) % 4, (y + o[1]) % 4, (z + o[2]) % 4, (core + o[3]) % 2)
+        dx, dy, dz, dc = o
+        return to_layer[dx][dc], zs[dz] * 8 + to_xy[dx][dy]
 
     def at(chunk):
         px, py, pz = chunk
@@ -80,14 +87,18 @@
     loads = []
     for k, chunk in enumerate(CHUNKS):
         zl, xl, yl = at(chunk)
-        load = pltpu.make_async_copy(kv_ref.at[:, :, :, zl, xl, :, yl], in_v.at[k], load_sem.at[k])
-        load.start()
-        loads.append(load)
+        loads.append(pltpu.make_async_copy(kv_ref.at[:, :, :, zl, xl, :, yl], in_v.at[k], load_sem.at[k]))
+    get_mask = pltpu.make_async_copy(mask_hbm, mask_ref, load_sem.at[9])
+    get_mask.start()
+    loads[0].start()
 
     barrier = pltpu.get_barrier_semaphore()
     for o in everyone:
         pl.semaphore_signal(barrier, inc=1, device_id=to(o), device_id_type=MESH)
+    for load in loads[1:]:
+        load.start()
 
+    get_mask.wait()
     limit = len_ref[0]
     square = (128, 128)
     diagonal = lax.broadcasted_iota(jnp.int32, square, 0) == lax.broadcasted_iota(jnp.int32, square, 1)
@@ -102,20 +113,26 @@
     slots = pl.ds(pl.multiple_of(tok * PAGE, PAGE), PAGE)
     here = out_ref.at[0, :, pl.ds(layer * 2, 2), :, slots, :]
 
-    def block(o):
-        there = to(o)
-        return there, buf.at[there[1] * 4 + there[0]]
+    def start(o, there):
+        data = buf.at[there[1] * 4 + there[0]]
+        if any(o):
+            pltpu.make_async_remote_copy(
+                src_ref=data, dst_ref=here, send_sem=send_sem, recv_sem=recv_sem,
+                device_id=there, device_id_type=MESH,
+            ).start()
+        else:
+            pltpu.make_async_copy(data, here, own_sem).start()
 
     def send(chunk):
         for o in sends_of(chunk):
-            there, data = block(o)
-            if any(o):
-                pltpu.make_async_remote_copy(
-                    src_ref=data, dst_ref=here, send_sem=send_sem, recv_sem=recv_sem,
-                    device_id=there, device_id_type=MESH,
-                ).start()
-            else:
-                pltpu.make_async_copy(data, here, own_sem).start()
+            start(o, to(o))
+
+    def send_last(chunk):
+        px, py, pz = chunk
+        for half, dc, sx, sy in itertools.product((0, 2), (0, 1), (0, 2), (0, 2)):
+            dx, dy = px + sx, py + sy
+            slot_z = lax.rem(z + pz, 2) + half
+            start(chunk, (to_layer[dx][dc], slot_z * 8 + to_xy[dx][dy]))
 
     for k, chunk in enumerate(CHUNKS):
         loads[k].wait()
@@ -125,9 +142,9 @@
             send(chunk)
         if k > 1:
             send(CHUNKS[k - 1])
-    send(CHUNKS[-1])
+    send_last(CHUNKS[-1])
 
-    pltpu.make_async_copy(block((0, 0, 0, 0))[1], here, own_sem).wait()
+    pltpu.make_async_copy(buf.at[tok * 4 + layer], here, own_sem).wait()
     rest = buf.at[pl.ds(0, 127)]
     pltpu.make_async_copy(rest, rest, send_sem).wait()
     pltpu.make_async_copy(rest, rest, recv_sem).wait()
@@ -149,16 +166,17 @@
         out_shape=pltpu.VMEM((1, 2, 8, 2, 512, HD), jnp.bfloat16),
         in_specs=[
             pl.BlockSpec(memory_space=pltpu.SMEM),
-            pl.BlockSpec(memory_space=pltpu.VMEM),
+            pl.BlockSpec(memory_space=pltpu.HBM),
             pl.BlockSpec(memory_space=pltpu.HBM),
         ],
         out_specs=pl.BlockSpec(memory_space=pltpu.VMEM),
         scratch_shapes=[
+            pltpu.VMEM((1, 512), jnp.int32),
             pltpu.VMEM((8, 2, 2, 2, 2, PAGE, KVH * HD), jnp.bfloat16),
             pltpu.VMEM((2, 2, 2, 2, 2, PAGE, HD), jnp.float32),
             pltpu.VMEM((2, 2, 2, 2, 2, PAGE, HD), jnp.float32),
             pltpu.VMEM((128, 2, 2, 2, PAGE, HD), jnp.bfloat16),
-            pltpu.SemaphoreType.DMA((8,)),
+            pltpu.SemaphoreType.DMA((10,)),
             pltpu.SemaphoreType.DMA,
             pltpu.SemaphoreType.DMA,
             pltpu.SemaphoreType.DMA,

time: 63.4 us -> 61 us (0.962)
  Pallas kernels: 62.4 us -> 60.3 us
    pallas_call x1, Pallas kernels: 60.2 us -> 58.1 us  [shards(): pl.pallas_call(kernel, out_shape=pltpu.VMEM((1, 2, 8, 2, 512, HD), jnp.bf...]
where the time goes in v3:
time: 61 us; the launch traced here: 60.9 us
  Pallas kernels  60.3 us (99%)
  between operations  0.66 us (1%)
    pallas_call x1, Pallas kernels, shards(): pl.pallas_call(kernel, out_shape=pltpu.VMEM((1, 2, 8, 2, 512, HD), jnp.bf...  58.1 us
    pallas_call x1, Pallas kernels, shards(): pl.pallas_call(put_out, out_shape=jax.ShapeDtypeStruct((1, 2, 8, 2, 512,...  2.14 us

profile of v3, /device:TPU:1, one launch (start us, length us, event | category | flops | bytes accessed | tf_op | source)
XLA Modules:
  0.0 60.9 jit_solution(17307598642149048926)
XLA Ops:
  0.7 58.1 %shard_map.37.in_ref = bf16[1,2,8,2,512,128]{5,4,3,2,1,0:T(8,128)(2,1)S(1)} custom-call(s32[1]{0:T(128)S(6)} %copy.4.len_ref, s32[1,512]{1,0:T(1,128)} %bitcast.3, bf16[2,2,2,2,2,2,2,16,1024]{8,7,6,5,4,3,2,1,0:T(8,128)(2,1)} %bitcast.2), custom_call_target="tpu_custom_call" | custom-call | tf_op jit(solution)/shard_map/pallas_call | solution.py:164
  58.8 2.1 %shard_map.38 = bf16[1,2,8,2,512,128]{5,4,3,2,1,0:T(8,128)(2,1)} custom-call(bf16[1,2,8,2,512,128]{5,4,3,2,1,0:T(8,128)(2,1)S(1)} %shard_map.37.in_ref), custom_call_target="tpu_custom_call" | custom-call | tf_op jit(solution)/shard_map/pallas_call | solution.py:186

commit v4 on v3

--- a/solution.py
+++ b/solution.py
@@ -13,7 +13,7 @@
 PAGE = 16
 EPS = 1e-06
 MESH = pl.DeviceIdType.MESH
-CHUNKS = [(1, 1, 1), (0, 0, 0), (0, 1, 1), (1, 0, 0), (1, 0, 1), (0, 1, 0), (1, 1, 0), (0, 0, 1)]
+CHUNKS = [(1, 1, 1), (0, 0, 0), (1, 0, 0), (0, 1, 1), (0, 1, 0), (1, 0, 1), (1, 1, 0), (0, 0, 1)]
 
 
 def place():

time: 61 us -> 60.8 us (level)
  no operation moved by 1% of the time
where the time goes in v4:
time: 60.8 us; the launch traced here: 60.7 us
  Pallas kernels  60.1 us (99%)
  between operations  0.66 us (1%)
    pallas_call x1, Pallas kernels, shards(): pl.pallas_call(kernel, out_shape=pltpu.VMEM((1, 2, 8, 2, 512, HD), jnp.bf...  57.9 us
    pallas_call x1, Pallas kernels, shards(): pl.pallas_call(put_out, out_shape=jax.ShapeDtypeStruct((1, 2, 8, 2, 512,...  2.14 us

profile of v4, /device:TPU:1, one launch (start us, length us, event | category | flops | bytes accessed | tf_op | source)
XLA Modules:
  0.0 60.7 jit_solution(8748100486775089664)
XLA Ops:
  0.7 57.9 %shard_map.37.in_ref = bf16[1,2,8,2,512,128]{5,4,3,2,1,0:T(8,128)(2,1)S(1)} custom-call(s32[1]{0:T(128)S(6)} %copy.4.len_ref, s32[1,512]{1,0:T(1,128)} %bitcast.3, bf16[2,2,2,2,2,2,2,16,1024]{8,7,6,5,4,3,2,1,0:T(8,128)(2,1)} %bitcast.2), custom_call_target="tpu_custom_call" | custom-call | tf_op jit(solution)/shard_map/pallas_call | solution.py:164
  58.6 2.1 %shard_map.38 = bf16[1,2,8,2,512,128]{5,4,3,2,1,0:T(8,128)(2,1)} custom-call(bf16[1,2,8,2,512,128]{5,4,3,2,1,0:T(8,128)(2,1)S(1)} %shard_map.37.in_ref), custom_call_target="tpu_custom_call" | custom-call | tf_op jit(solution)/shard_map/pallas_call | solution.py:186
